TPU v7x, 32 devices: a whole 2x2x4 slice. The times are simulated.
32 devices in a mesh: layer: 2 (over y), feat: 4 (over x, core), width: 4 (over z).
Axes of the slice: x: 2, y: 2, z: 4, core: 2. Of those that a mesh axis runs over, the one named last changes fastest.
Arguments:
- resid: bfloat16 [2, 128, 2048], P(None, 'layer', 'width'), may hold values from -6 to 6
- enc_w: bfloat16 [2, 2048, 65536], P(None, 'width', ('layer', 'feat')), may hold values from -0.125 to 0.125
- enc_b: float32 [2, 65536], P(None, ('layer', 'feat')), may hold values from -3 to 3
- dec_w: float32 [3, 65536, 2048], P(None, ('layer', 'feat'), 'width'), may hold values from -0.03125 to 0.03125
- dec_b: float32 [2, 2048], P(None, 'width'), may hold values from -2 to 2
- target: float32 [2, 128, 2048], P(None, ('layer', 'feat'), 'width'), may hold values from -6 to 6
Outputs:
- recon: float32 [2, 128, 2048], P(None, ('layer', 'feat'), 'width')
- err: float32 [2, 128], P(None, ('layer', 'feat'))
All inputs are finite; a program needn't handle non-finite values.
Results may differ from a plain program's by a relative error of at most 0.00035.
Values may be sent and summed in bfloat16 or wider, within the bound.
No kernel may reach another device: no remote copies, remote signals or barrier semaphores. Data moves between devices by JAX's collectives and lax.ppermute only.
A program may use at most 128 MiB of HBM per device.

v0:
```python
import jax
import jax.numpy as jnp
from jax import lax
from jax.sharding import PartitionSpec as P


def decode_rows(act, dec_w, target_idx):
    total = None
    for layer_idx in range(target_idx + 1):
        block = target_idx * (target_idx + 1) // 2 + layer_idx
        rows = act[layer_idx]
        term = jnp.dot(
            rows, dec_w[block], precision=lax.Precision.HIGHEST, preferred_element_type=jnp.float32
        )
        total = term if total is None else total + term
    return total


def per_device(resid, enc_w, enc_b, dec_w, dec_b, target):
    layers = resid.shape[0]
    gathered = lax.all_gather(resid, "layer", axis=1, tiled=True)
    tokens = gathered.shape[1]
    partial_pre = jnp.einsum("ltd,ldf->ltf", gathered, enc_w, preferred_element_type=jnp.float32)
    pre = lax.psum(partial_pre, "width")
    act = jnp.maximum(pre + enc_b[:, None, :], 0.0)
    own_rows = tokens // lax.axis_size(("layer", "feat"))
    summed = lax.psum_scatter(
        jnp.concatenate(
            [decode_rows(act, dec_w, target_idx) for target_idx in range(layers)], axis=1
        ),
        ("layer", "feat"),
        scatter_dimension=0,
        tiled=True,
    )
    summed = summed.reshape(own_rows, layers, dec_w.shape[2]).transpose(1, 0, 2)
    recon = summed + dec_b[:, None, :]
    diff = recon - target
    sq_error, sq_target = lax.psum(
        (jnp.sum(diff * diff, axis=2), jnp.sum(target * target, axis=2)), "width"
    )
    err = sq_error / (sq_target + 1e-06)
    return (recon, err)


def solution(mesh):
    in_specs = (
        P(None, "layer", "width"),
        P(None, "width", ("layer", "feat")),
        P(None, ("layer", "feat")),
        P(None, ("layer", "feat"), "width"),
        P(None, "width"),
        P(None, ("layer", "feat"), "width"),
    )
    out_specs = (P(None, ("layer", "feat"), "width"), P(None, ("layer", "feat")))
    return jax.shard_map(
        per_device, mesh=mesh, in_specs=in_specs, out_specs=out_specs, check_vma=False
    )
```

profile of v0, /device:TPU:0, one launch (start us, length us, event | category | flops | bytes accessed | tf_op | source)
XLA Modules:
  0.0 413.2 jit_solution(15221711624656479680)
XLA Ops:
  7.2 0.0 all-reduce.3.cloned.1.call-start
  7.2 7.4 %all_gather.3 = bf16[2,128,512]{2,1,0:T(8,128)(2,1)S(1)} all-gather(bf16[2,64,512]{2,1,0:T(8,128)(2,1)} %param.6), channel_id=1, replica_groups=mesh['layer'=2,'feat'=4,'width'=4] {'layer'}, dimensions={1}, use_global_device_ids=true | all-gather | bytes 393216 | tf_op jit(solution)/shard_map/all_gather | solution.py:21
  14.6 11.3 %fusion.14 = f32[2,128,8192]{2,1,0:T(8,128)} fusion(bf16[2,128,512]{2,1,0:T(8,128)(2,1)S(1)} %all_gather.3, bf16[2,512,8192]{2,1,0:T(8,128)(2,1)} %param.7), kind=kOutput, calls=%fused_computation.19 | convolution fusion | flops 2147483648 | bytes 25427968 | tf_op jit(solution)/shard_map/ltd,ldf->ltf/dot_general | solution.py:23
  26.0 0.0 copy-start
  26.0 0.0 all-reduce.3.cloned.1.call-update
  26.0 0.0 reduce-scatter.2.cloned.1.call-start
  26.0 292.4 %all-reduce.3.cloned.1.call-done = f32[2,128,8192]{2,1,0:T(8,128)} async-done(((f32[2,128,8192]{2,1,0:T(8,128)}), f32[2,128,8192]{2,1,0:T(8,128)}) %all-reduce.3.cloned.1.call-update) | async-done | bytes 8388624 | tf_op jit(solution)/shard_map/psum | solution.py:24
  318.4 0.0 copy-done
  318.4 4.2 %add_maximum_fusion = f32[2,128,8192]{2,1,0:T(8,128)S(1)} fusion(f32[2,128,8192]{2,1,0:T(8,128)} %all-reduce.3.cloned.1.call-done, f32[2,8192]{1,0:T(2,128)S(1)} %copy-done), kind=kLoop, calls=%fused_computation.9 | loop fusion | flops 4194304 | bytes 16842752 | tf_op jit(solution)/shard_map/max | solution.py:25
  322.6 11.9 %fusion = f32[128,512]{1,0:T(8,128)S(1)} fusion(f32[3,8192,512]{2,1,0:T(8,128)} %param.9, f32[2,128,8192]{2,1,0:T(8,128)S(1)} %add_maximum_fusion), kind=kOutput, calls=%fused_computation | convolution fusion | flops 6442450944 | bytes 21233664 | tf_op jit(solution)/shard_map/dot_general | solution.py:12
  334.5 11.9 %fusion.4 = f32[128,512]{1,0:T(8,128)S(1)} fusion(f32[3,8192,512]{2,1,0:T(8,128)} %param.9, f32[2,128,8192]{2,1,0:T(8,128)S(1)} %add_maximum_fusion), kind=kOutput, calls=%fused_computation.4 | convolution fusion | flops 6442450944 | bytes 21233664 | tf_op jit(solution)/shard_map/dot_general | solution.py:12
  346.4 0.0 copy-start.1
  346.4 0.0 copy-start.2
  346.4 12.1 %fusion.9 = f32[128,512]{1,0:T(8,128)S(1)} fusion(f32[128,512]{1,0:T(8,128)S(1)} %fusion, f32[3,8192,512]{2,1,0:T(8,128)} %param.9, f32[2,128,8192]{2,1,0:T(8,128)S(1)} %add_maximum_fusion), kind=kOutput, calls=%fused_computation.12 | convolution fusion | flops 6442516480 | bytes 21495808 | tf_op jit(solution)/shard_map/dot_general | solution.py:12
  358.5 0.8 pad_maximum_fusion
  359.3 0.0 reduce-scatter.2.cloned.1.call-update
  359.4 33.2 %reduce-scatter.2.cloned.1.call-done = f32[16,1024]{1,0:T(8,128)} async-done(((f32[128,1024]{1,0:T(8,128)}), f32[16,1024]{1,0:T(8,128)}) %reduce-scatter.2.cloned.1.call-update) | async-done | bytes 65552 | tf_op jit(solution)/shard_map/reduce_scatter | solution.py:27
  392.6 0.0 copy-done.1
  392.6 0.0 copy-done.2
  392.6 1.5 multiply_reduce_fusion
  394.1 11.6 %all-reduce = (f32[2,16]{1,0:T(2,128)S(1)}, f32[2,16]{1,0:T(2,128)S(1)}) all-reduce(f32[2,16]{1,0:T(2,128)S(1)} %get-tuple-element.3, f32[2,16]{1,0:T(2,128)S(1)} %get-tuple-element.2), channel_id=1, replica_groups=mesh['layer'=2,'feat'=4,'width'=4] {'width'}, use_global_device_ids=true, to_apply=%region_3.0 | all-reduce | flops 64 | bytes 512 | tf_op jit(solution)/shard_map/psum | solution.py:38
  405.8 0.6 add_divide_fusion
Async XLA Ops:
  7.2 311.2 %all-reduce.3.cloned.1.call-start = ((), (), s32[]{:S(2)}) async-start(), calls=%async_computation.1 | async-start | bytes 16777216 | tf_op jit(solution)/shard_map/psum | solution.py:24
  26.0 292.4 %copy-start = (f32[2,8192]{1,0:T(2,128)S(1)}, f32[2,8192]{1,0:T(2,128)}, u32[]{:S(2)}) copy-start(f32[2,8192]{1,0:T(2,128)} %param.8) | copy-start | bytes 196612
  26.0 366.6 %reduce-scatter.2.cloned.1.call-start = ((), (), s32[]{:S(2)}) async-start(), calls=%async_computation.2 | async-start | bytes 589824 | tf_op jit(solution)/shard_map/reduce_scatter | solution.py:27
  346.4 46.2 %copy-start.1 = (f32[2,16,512]{2,1,0:T(8,128)S(1)}, f32[2,16,512]{2,1,0:T(8,128)}, u32[]{:S(2)}) copy-start(f32[2,16,512]{2,1,0:T(8,128)} %param.11) | copy-start | bytes 196612
  346.4 46.2 %copy-start.2 = (f32[2,512]{1,0:T(2,128)S(1)}, f32[2,512]{1,0:T(2,128)}, u32[]{:S(2)}) copy-start(f32[2,512]{1,0:T(2,128)} %param.10) | copy-start | bytes 12292
Sparse Core Ops, SparseCore 0:
  26.1 292.2 all-reduce.2
  359.5 33.0 reduce-scatter.1
where the time goes:
time: 413 us
  waiting for transfers between devices  326 us (79%)
  matrix products  47.2 us (11%)
  blocking collectives  19.1 us (5%)
  between operations  14.1 us (3%)
  other arithmetic  7.07 us (2%)
    psum x1, waiting for transfers between devices, per_device(): pre = lax.psum(partial_pre, 'width')  292 us
    dot_general x3, matrix products, decode_rows(): jnp.dot(rows, dec_w[block], precision=lax.Precision.HIGHEST, preferred_el...  35.9 us
    reduce_scatter x1, waiting for transfers between devices, per_device(): lax.psum_scatter(jnp.concatenate([decode_rows(act, dec_w, target_idx) for...  33.2 us
    psum x1, blocking collectives, per_device(): lax.psum((jnp.sum(diff * diff, axis=2), jnp.sum(target * target, axis=2))...  11.6 us
    dot_general x1, matrix products, per_device(): jnp.einsum('ltd,ldf->ltf', gathered, enc_w, preferred_element_type=jnp.fl...  11.3 us
  transfers between devices with their start and end apart: 2, of which 2 were waited for; matrix products, arithmetic and copies ran while one was open for 0% of the time, Pallas kernels for 0%

commit v1 on v0

--- a/solution.py
+++ b/solution.py
@@ -21,7 +21,7 @@
     gathered = lax.all_gather(resid, "layer", axis=1, tiled=True)
     tokens = gathered.shape[1]
     partial_pre = jnp.einsum("ltd,ldf->ltf", gathered, enc_w, preferred_element_type=jnp.float32)
-    pre = lax.psum(partial_pre, "width")
+    pre = jnp.sum(lax.all_gather(partial_pre, "width"), axis=0)
     act = jnp.maximum(pre + enc_b[:, None, :], 0.0)
     own_rows = tokens // lax.axis_size(("layer", "feat"))
     summed = lax.psum_scatter(

time: 413 us -> 699 us (1.69)
  waiting for transfers between devices: 326 us -> 595 us
  other arithmetic: 7.07 us -> 22.7 us
    all_gather x0 -> x1, waiting for transfers between devices: none -> 563 us  [per_device(): pre = jnp.sum(lax.all_gather(partial_pre, 'width'), axis=0)]
    psum x1 -> x0, waiting for transfers between devices: 292 us -> none  [per_device(): pre = lax.psum(partial_pre, 'width')]
    reduce_sum x0 -> x1, other arithmetic: none -> 15.7 us  [per_device(): pre = jnp.sum(lax.all_gather(partial_pre, 'width'), axis=0)]
where the time goes in v1:
time: 699 us
  waiting for transfers between devices  595 us (85%)
  matrix products  47.2 us (7%)
  other arithmetic  22.7 us (3%)
  blocking collectives  19.1 us (3%)
  between operations  14.1 us (2%)
    all_gather x1, waiting for transfers between devices, per_device(): pre = jnp.sum(lax.all_gather(partial_pre, 'width'), axis=0)  563 us
    dot_general x3, matrix products, decode_rows(): jnp.dot(rows, dec_w[block], precision=lax.Precision.HIGHEST, preferred_el...  35.9 us
    reduce_scatter x1, waiting for transfers between devices, per_device(): lax.psum_scatter(jnp.concatenate([decode_rows(act, dec_w, target_idx) for...  32.5 us
    reduce_sum x1, other arithmetic, per_device(): pre = jnp.sum(lax.all_gather(partial_pre, 'width'), axis=0)  15.7 us
  transfers between devices with their start and end apart: 2, of which 2 were waited for; matrix products, arithmetic and copies ran while one was open for 0% of the time, Pallas kernels for 0%

profile of v1, /device:TPU:0, one launch (start us, length us, event | category | flops | bytes accessed | tf_op | source)
XLA Modules:
  0.0 698.6 jit_solution(2223347936660237197)
XLA Ops:
  7.2 0.0 all-gather.3.cloned.1.call-start
  7.2 7.4 %all_gather.9 = bf16[2,128,512]{2,1,0:T(8,128)(2,1)S(1)} all-gather(bf16[2,64,512]{2,1,0:T(8,128)(2,1)} %param.6), channel_id=1, replica_groups=mesh['layer'=2,'feat'=4,'width'=4] {'layer'}, dimensions={1}, use_global_device_ids=true | all-gather | bytes 393216 | tf_op jit(solution)/shard_map/all_gather | solution.py:21
  14.6 11.3 %fusion.14 = f32[2,128,8192]{2,1,0:T(8,128)} fusion(bf16[2,128,512]{2,1,0:T(8,128)(2,1)S(1)} %all_gather.9, bf16[2,512,8192]{2,1,0:T(8,128)(2,1)} %param.7), kind=kOutput, calls=%fused_computation.19 | convolution fusion | flops 2147483648 | bytes 25427968 | tf_op jit(solution)/shard_map/ltd,ldf->ltf/dot_general | solution.py:23
  26.0 0.0 all-gather.3.cloned.1.call-update
  26.0 0.2 reduce-scatter.2.cloned.1.call-start
  26.2 562.7 %all-gather.3.cloned.1.call-done = f32[8,128,8192]{2,1,0:T(8,128)} async-done(((f32[2,128,8192]{2,1,0:T(8,128)}), f32[8,128,8192]{2,1,0:T(8,128)}) %all-gather.3.cloned.1.call-update) | async-done | bytes 33554448 | tf_op jit(solution)/shard_map/all_gather | solution.py:24
  588.9 0.0 copy-start
  588.9 15.7 %reduce_sum.27 = f32[2,128,8192]{2,1,0:T(8,128)} reduce(f32[4,2,128,8192]{3,2,1,0:T(8,128)} %bitcast.32, f32[]{:T(128)} %constant.2.clone.1), dimensions={0}, to_apply=%region_0.0 | reduce | flops 6291456 | bytes 41943044 | tf_op jit(solution)/shard_map/reduce_sum | solution.py:24
  604.6 0.0 copy-done
  604.6 4.2 add_maximum_fusion
  608.8 11.9 %fusion = f32[128,512]{1,0:T(8,128)S(1)} fusion(f32[3,8192,512]{2,1,0:T(8,128)} %param.9, f32[2,128,8192]{2,1,0:T(8,128)S(1)} %add_maximum_fusion), kind=kOutput, calls=%fused_computation | convolution fusion | flops 6442450944 | bytes 21233664 | tf_op jit(solution)/shard_map/dot_general | solution.py:12
  620.7 11.9 %fusion.4 = f32[128,512]{1,0:T(8,128)S(1)} fusion(f32[3,8192,512]{2,1,0:T(8,128)} %param.9, f32[2,128,8192]{2,1,0:T(8,128)S(1)} %add_maximum_fusion), kind=kOutput, calls=%fused_computation.4 | convolution fusion | flops 6442450944 | bytes 21233664 | tf_op jit(solution)/shard_map/dot_general | solution.py:12
  632.6 0.0 copy-start.1
  632.6 0.0 copy-start.2
  632.6 12.1 %fusion.9 = f32[128,512]{1,0:T(8,128)S(1)} fusion(f32[128,512]{1,0:T(8,128)S(1)} %fusion, f32[3,8192,512]{2,1,0:T(8,128)} %param.9, f32[2,128,8192]{2,1,0:T(8,128)S(1)} %add_maximum_fusion), kind=kOutput, calls=%fused_computation.12 | convolution fusion | flops 6442516480 | bytes 21495808 | tf_op jit(solution)/shard_map/dot_general | solution.py:12
  644.8 0.8 pad_maximum_fusion
  645.6 0.0 reduce-scatter.2.cloned.1.call-update
  645.6 32.5 %reduce-scatter.2.cloned.1.call-done = f32[16,1024]{1,0:T(8,128)} async-done(((f32[128,1024]{1,0:T(8,128)}), f32[16,1024]{1,0:T(8,128)}) %reduce-scatter.2.cloned.1.call-update) | async-done | bytes 65552 | tf_op jit(solution)/shard_map/reduce_scatter | solution.py:27
  678.1 0.0 copy-done.1
  678.1 0.0 copy-done.2
  678.1 1.5 multiply_reduce_fusion
  679.6 11.6 %all-reduce = (f32[2,16]{1,0:T(2,128)S(1)}, f32[2,16]{1,0:T(2,128)S(1)}) all-reduce(f32[2,16]{1,0:T(2,128)S(1)} %get-tuple-element.3, f32[2,16]{1,0:T(2,128)S(1)} %get-tuple-element.2), channel_id=1, replica_groups=mesh['layer'=2,'feat'=4,'width'=4] {'width'}, use_global_device_ids=true, to_apply=%region_3.0 | all-reduce | flops 64 | bytes 512 | tf_op jit(solution)/shard_map/psum | solution.py:38
  691.2 0.6 add_divide_fusion
Async XLA Ops:
  7.2 581.8 %all-gather.3.cloned.1.call-start = ((), (), s32[]{:S(2)}) async-start(), calls=%async_computation.2 | async-start | bytes 41943040 | tf_op jit(solution)/shard_map/all_gather | solution.py:24
  26.0 652.1 %reduce-scatter.2.cloned.1.call-start = ((), (), s32[]{:S(2)}) async-start(), calls=%async_computation.1 | async-start | bytes 589824 | tf_op jit(solution)/shard_map/reduce_scatter | solution.py:27
  588.9 15.7 %copy-start = (f32[2,8192]{1,0:T(2,128)S(1)}, f32[2,8192]{1,0:T(2,128)}, u32[]{:S(2)}) copy-start(f32[2,8192]{1,0:T(2,128)} %param.8) | copy-start | bytes 196612
  632.6 45.5 %copy-start.1 = (f32[2,16,512]{2,1,0:T(8,128)S(1)}, f32[2,16,512]{2,1,0:T(8,128)}, u32[]{:S(2)}) copy-start(f32[2,16,512]{2,1,0:T(8,128)} %param.11) | copy-start | bytes 196612
  632.6 45.5 %copy-start.2 = (f32[2,512]{1,0:T(2,128)S(1)}, f32[2,512]{1,0:T(2,128)}, u32[]{:S(2)}) copy-start(f32[2,512]{1,0:T(2,128)} %param.10) | copy-start | bytes 12292
Sparse Core Ops, SparseCore 0:
  26.1 562.7 all-gather.2
  645.7 32.2 reduce-scatter.1
